TPU v7x, 32 devices: a whole 2x2x4 slice. The times are simulated.
32 devices in a mesh: mem: 4 (over y, x), lat: 8 (over z, core).
Axes of the slice: x: 2, y: 2, z: 4, core: 2. Of those that a mesh axis runs over, the one named last changes fastest.
Arguments:
- gradient: float32 [2, 4, 192, 256], P(None, 'mem', 'lat'), may hold values from -24 to 24
- perturbations: bfloat16 [16, 2, 4, 192, 256], P('mem', None, None, 'lat'), may hold values from -6 to 6
- weights: float32 [16, 4, 192, 256], P('mem', None, 'lat'), may hold values from -6 to 6
- lon_taps: float32 [25], replicated, may hold values from 0.05 to 0.3
- lat_taps: float32 [25], replicated, may hold values from 0.05 to 0.3
- lev_taps: float32 [5], replicated, may hold values from 0.2 to 0.7
- level_order: int32 [4], replicated, may hold values from 0 to 3, each once
Outputs:
- updated_weights: float32 [16, 4, 192, 256], P('mem', None, 'lat')
- increment: float32 [2, 4, 192, 256], P(None, 'mem', 'lat')
Inputs may be any that keep to these rules, and one draw needn't show every extreme that they name: `level_order`: each level appears in exactly one slot.
All inputs are finite; a program needn't handle non-finite values.
Results may differ from a plain program's by a relative error of at most 0.0003.
Values sent between devices are 32-bit elements; how exact they have to be, the bound alone decides.
A program may use at most 128 MiB of HBM per device.

v0:
```python
import math

import jax
import jax.numpy as jnp
from jax import lax
from jax.sharding import PartitionSpec as P

STEP_RATE = 0.5


def with_halo(block, sides, width):
    for axis, dim in sides:
        count = lax.axis_size(axis)
        forward = [(i, i + 1) for i in range(count - 1)]
        backward = [(target, source) for source, target in forward]
        low = lax.ppermute(
            lax.slice_in_dim(block, block.shape[dim] - width, None, axis=dim), axis, forward
        )
        high = lax.ppermute(lax.slice_in_dim(block, 0, width, axis=dim), axis, backward)
        block = jnp.concatenate([low, block, high], axis=dim)
    return block


def circulant(tap_weights, longitudes):
    radius = tap_weights.shape[0] // 2
    row_index = lax.broadcasted_iota(jnp.int32, (longitudes, longitudes), 0)
    col_index = lax.broadcasted_iota(jnp.int32, (longitudes, longitudes), 1)
    offsets = (row_index - col_index + radius) % longitudes
    matrix = jnp.zeros((longitudes, longitudes), jnp.float32)
    for position in range(tap_weights.shape[0]):
        matrix = jnp.where(offsets == position, tap_weights[position], matrix)
    return matrix


def lat_forward(extended, tap_weights):
    width = tap_weights.shape[0]
    out_rows = extended.shape[-2] - width + 1
    result = tap_weights[0] * lax.slice_in_dim(extended, 0, out_rows, axis=extended.ndim - 2)
    for position in range(1, width):
        result = result + tap_weights[position] * lax.slice_in_dim(
            extended, position, position + out_rows, axis=extended.ndim - 2
        )
    return result


def lat_adjoint(extended, tap_weights):
    width = tap_weights.shape[0]
    out_rows = extended.shape[-2] - width + 1
    result = tap_weights[0] * lax.slice_in_dim(
        extended, width - 1, width - 1 + out_rows, axis=extended.ndim - 2
    )
    for position in range(1, width):
        start_row = width - 1 - position
        result = result + tap_weights[position] * lax.slice_in_dim(
            extended, start_row, start_row + out_rows, axis=extended.ndim - 2
        )
    return result


def pad_levels(values, amount):
    widths = [(0, 0)] * values.ndim
    widths[values.ndim - 3] = (amount, amount)
    return jnp.pad(values, widths)


def level_filter(values, tap_weights, flipped):
    width = tap_weights.shape[0]
    padded = pad_levels(values, width // 2)
    levels = values.shape[-3]
    result = jnp.zeros_like(values)
    for position in range(width):
        start_level = width - 1 - position if flipped else position
        result = result + tap_weights[position] * lax.slice_in_dim(
            padded, start_level, start_level + levels, axis=padded.ndim - 3
        )
    return result


def on_device(gradient, perturbations, weights, lon_taps, lat_taps, lev_taps, level_order):
    radius = lat_taps.shape[0] // 2
    local_members, levels, band_rows, longitudes = weights.shape
    members = local_members * lax.axis_size("mem")
    norm_factor = 1.0 / math.sqrt(members - 1)
    slot_blocks = lax.all_gather(gradient, "mem", axis=1, tiled=True)
    onehot = (level_order[:, None] == jnp.arange(levels, dtype=jnp.int32)[None, :]).astype(
        jnp.float32
    )
    grad_levels = jnp.einsum("sl,vsyx->vlyx", onehot, slot_blocks, precision=lax.Precision.HIGHEST)
    products = norm_factor * (
        perturbations[:, 0] * grad_levels[0] + perturbations[:, 1] * grad_levels[1]
    )
    matrix = circulant(lon_taps, longitudes)
    filtered = level_filter(
        jnp.einsum("...m,im->...i", products, matrix, precision=lax.Precision.HIGHEST),
        lev_taps,
        True,
    )
    extended = with_halo(filtered, (("lat", 2),), radius)
    adjoint = lat_adjoint(extended, lat_taps)
    grad_total = weights + adjoint
    updated = weights - STEP_RATE * grad_total / (1.0 + jnp.abs(grad_total))
    widened = with_halo(updated, (("lat", 2),), radius)
    grid_field = level_filter(
        jnp.einsum(
            "...m,mi->...i", lat_forward(widened, lat_taps), matrix, precision=lax.Precision.HIGHEST
        ),
        lev_taps,
        False,
    )
    increment = norm_factor * jnp.sum(perturbations * grid_field[:, None], axis=0)
    slot_sums = jnp.einsum("sl,vlyx->vsyx", onehot, increment, precision=lax.Precision.HIGHEST)
    owned = lax.psum_scatter(slot_sums, "mem", scatter_dimension=1, tiled=True)
    return (updated, owned)


def solution(mesh):
    in_specs = (
        P(None, "mem", "lat", None),
        P("mem", None, None, "lat", None),
        P("mem", None, "lat", None),
        P(),
        P(),
        P(),
        P(),
    )
    out_specs = (P("mem", None, "lat", None), P(None, "mem", "lat", None))
    return jax.shard_map(
        on_device, mesh=mesh, in_specs=in_specs, out_specs=out_specs, check_vma=False
    )
```

profile of v0, /device:TPU:0, one launch (start us, length us, event | category | flops | bytes accessed | tf_op | source)
XLA Modules:
  0.0 148.8 jit_solution(5196891547863798654)
XLA Ops:
  7.2 0.0 reduce-scatter.4.cloned.1.call-start
  7.2 0.0 copy-start.3
  7.2 1.6 %fusion.295 = (f32[1]{0:T(128)}, f32[1]{0:T(128)}, f32[1]{0:T(128)}, f32[1]{0:T(128)}, f32[1]{0:T(128)}, /*index=5*/f32[1]{0:T(128)}) fusion(f32[25]{0:T(128)} %param.10), kind=kLoop, calls=%fused_computation.382 | loop fusion | bytes 48 | tf_op jit(solution)/shard_map/slice | solution.py:31
  8.8 0.0 copy-done.3
  8.8 0.0 copy-start.5
  8.8 0.7 fusion.294
  9.5 0.0 copy-done.5
  9.5 0.7 fusion.293
  10.2 0.0 copy-start.6
  10.2 10.6 %all_gather.3 = f32[2,4,24,256]{3,2,0,1:T(8,128)S(1)} all-gather(f32[2,1,24,256]{3,2,0,1:T(8,128)} %bitcast.94), channel_id=1, replica_groups=mesh['mem'=4,'lat'=8] {'mem'}, dimensions={1}, use_global_device_ids=true | all-gather | bytes 245760 | tf_op jit(solution)/shard_map/all_gather | solution.py:84
  20.8 0.0 copy-done.6
  20.8 0.5 convolution_bitcast_fusion.1
  21.3 0.0 copy-start.2
  21.4 0.9 copy-done.2
  22.3 16.7 %fusion.186 = f32[4,4,24,256]{3,2,1,0:T(8,128)S(1)} fusion(f32[4,24,256]{2,1,0:T(8,128)S(1)} %copy.20, bf16[4,2,4,24,256]{4,3,2,1,0:T(8,128)(2,1)S(1)} %copy-done.2, f32[4,24,256]{2,1,0:T(8,128)S(1)} %copy.18, f32[]{:T(128)} %bitcast.33, f32[]{:T(128)} %bitcast.32, f32[]{:T(128)} %bitcast.31, f32[]{:T(128)} %bitcast.30, f32[]{:T(128)} %bitcast.29, ...), kind=kOutput, calls=%fused_computation.266 | convolution fusion | flops 306708480 | bytes 983140 | tf_op jit(solution)/shard_map/...m,im->...i/dot_general | solution.py:94
  39.0 3.2 %fusion.4 = f32[4,4,24,256]{3,2,1,0:T(8,128)S(1)} fusion(f32[4,4,24,256]{3,2,1,0:T(8,128)S(1)} %fusion.186, f32[]{:T(128)} %bitcast.39, f32[]{:T(128)} %bitcast.38, f32[]{:T(128)} %bitcast.37, f32[]{:T(128)} %bitcast.36, f32[]{:T(128)} %bitcast.1), kind=kLoop, calls=%fused_computation.103 | loop fusion | flops 884736 | bytes 786452 | tf_op jit(solution)/shard_map/add | solution.py:73
  42.2 0.0 copy-start.1
  42.3 0.0 copy-start.4
  42.3 1.4 collective-permute-start
  43.7 3.0 %collective-permute-start.1 = (f32[4,4,12,256]{3,2,1,0:T(8,128)S(1)}, f32[4,4,12,256]{3,2,1,0:T(8,128)S(1)}, u32[]{:S(2)}, u32[]{:S(2)}) collective-permute-start(f32[4,4,12,256]{3,2,1,0:T(8,128)S(1)} %get-tuple-element.9), channel_id=1, source_target_pairs={{0,1},{1,2},{2,3},{3,4},{4,5},{5,6},{6,7},{8,9},{9,10},{10,11},{11... | collective-permute-start | bytes 589832 | tf_op jit(solution)/shard_map/ppermute | solution.py:16
  46.8 0.0 copy-done.4
  46.8 0.7 fusion.292
  47.5 0.7 fusion.291
  48.2 0.0 collective-permute-done
  48.2 0.0 collective-permute-done.1
  48.2 0.0 copy-done.1
  48.2 17.3 %divide_subtract_fusion = f32[4,4,24,256]{3,2,1,0:T(8,128)S(1)} fusion(f32[4,4,24,256]{3,2,1,0:T(8,128)S(1)} %copy-done.1, f32[4,4,24,256]{3,2,1,0:T(8,128)S(1)} %fusion.4, f32[4,4,12,256]{3,2,1,0:T(8,128)S(1)} %collective-permute-done.1, f32[4,4,12,256]{3,2,1,0:T(8,128)S(1)} %collective-permute-done, f32[]{:T(128)} %bitcast.63, f32[]{:T(128)} %bitcast.62, ...), kind=kLoop, calls=%fused_computation.269 | loop fusion | flops 7766016 | bytes 1572964 | tf_op jit(solution)/shard_map/sub | solution.py:101
  65.5 0.0 copy-start
  65.6 5.0 %collective-permute-start.2 = (f32[4,4,12,256]{3,2,1,0:T(8,128)S(1)}, f32[4,4,12,256]{3,2,1,0:T(8,128)S(1)}, u32[]{:S(2)}, u32[]{:S(2)}) collective-permute-start(f32[4,4,12,256]{3,2,1,0:T(8,128)S(1)} %get-tuple-element.6), channel_id=1, source_target_pairs={{0,1},{1,2},{2,3},{3,4},{4,5},{5,6},{6,7},{8,9},{9,10},{10,11},{11... | collective-permute-start | bytes 589832 | tf_op jit(solution)/shard_map/ppermute | solution.py:16
  70.5 1.3 collective-permute-start.3
  71.8 0.0 collective-permute-done.2
  71.9 4.1 %collective-permute-done.3 = f32[4,4,12,256]{3,2,1,0:T(8,128)S(1)} collective-permute-done((f32[4,4,12,256]{3,2,1,0:T(8,128)S(1)}, f32[4,4,12,256]{3,2,1,0:T(8,128)S(1)}, u32[]{:S(2)}, u32[]{:S(2)}) %collective-permute-start.3) | collective-permute-done | bytes 196640 | tf_op jit(solution)/shard_map/ppermute | solution.py:19
  75.9 0.0 copy-done
  75.9 33.5 %fusion.20 = f32[4,4,24,256]{3,2,1,0:T(8,128)S(1)} fusion(f32[4,4,24,256]{3,2,1,0:T(8,128)S(1)} %divide_subtract_fusion, f32[4,4,12,256]{3,2,1,0:T(8,128)S(1)} %collective-permute-done.3, f32[4,4,12,256]{3,2,1,0:T(8,128)S(1)} %collective-permute-done.2, f32[]{:T(128)} %bitcast.63, f32[]{:T(128)} %bitcast.62, f32[]{:T(128)} %bitcast.61, f32[]{:T(128)} %bitcast.60, ...), kind=kOutput, calls=%fused_computation.119 | convolution fusion | flops 313294848 | bytes 1179848 | tf_op jit(solution)/shard_map/...m,mi->...i/dot_general | solution.py:104
  109.5 3.2 %fusion.12 = f32[4,4,24,256]{3,2,1,0:T(8,128)S(1)} fusion(f32[4,4,24,256]{3,2,1,0:T(8,128)S(1)} %fusion.20, f32[]{:T(128)} %bitcast.39, f32[]{:T(128)} %bitcast.38, f32[]{:T(128)} %bitcast.37, f32[]{:T(128)} %bitcast.36, f32[]{:T(128)} %bitcast.1), kind=kLoop, calls=%fused_computation.111 | loop fusion | flops 884736 | bytes 786452 | tf_op jit(solution)/shard_map/add | solution.py:73
  112.7 0.1 multiply_reduce_fusion
  112.8 0.4 convolution_bitcast_fusion
  113.2 0.7 copy.22
  113.9 0.0 reduce-scatter.4.cloned.1.call-update
  113.9 28.0 %reduce-scatter.4.cloned.1.call-done = f32[2,1,24,256]{3,2,0,1:T(8,128)} async-done(((f32[2,4,24,256]{3,2,0,1:T(8,128)}), f32[2,1,24,256]{3,2,0,1:T(8,128)}) %reduce-scatter.4.cloned.1.call-update) | async-done | bytes 49168
  (6 shorter events, 0.2 us)
Async XLA Ops:
  7.2 134.8 %reduce-scatter.4.cloned.1.call-start = ((), (), s32[]{:S(2)}) async-start(), calls=%async_computation.1 | async-start | bytes 245760
  7.2 1.6 %copy-start.3 = (f32[25]{0:T(128)S(1)}, f32[25]{0:T(128)}, u32[]{:S(2)}) copy-start(f32[25]{0:T(128)} %param.10) | copy-start | bytes 304
  8.8 0.7 copy-start.5
  10.2 10.6 %copy-start.6 = (s32[4]{0:T(128)S(1)}, s32[4]{0:T(128)}, u32[]{:S(2)}) copy-start(s32[4]{0:T(128)} %param.13) | copy-start | bytes 52
  21.3 1.0 copy-start.2
  42.2 6.0 %copy-start.1 = (f32[4,4,24,256]{3,2,1,0:T(8,128)S(1)}, f32[4,4,24,256]{3,2,1,0:T(8,128)}, u32[]{:S(2)}) copy-start(f32[4,4,24,256]{3,2,1,0:T(8,128)} %param.9) | copy-start | bytes 1179652
  42.3 4.5 %copy-start.4 = (f32[25]{0:T(128)S(1)}, f32[25]{0:T(128)}, u32[]{:S(2)}) copy-start(f32[25]{0:T(128)} %param.11) | copy-start | bytes 304
  42.3 5.9 %collective-permute-start = (f32[4,4,12,256]{3,2,1,0:T(8,128)S(1)}, f32[4,4,12,256]{3,2,1,0:T(8,128)S(1)}, u32[]{:S(2)}, u32[]{:S(2)}) collective-permute-start(f32[4,4,12,256]{3,2,1,0:T(8,128)S(1)} %get-tuple-element.8), channel_id=1, source_target_pairs={{1,0},{2,1},{3,2},{4,3},{5,4},{6,5},{7,6},{9,8},{10,9},{11,10},{12... | collective-permute-start | bytes 589832 | tf_op jit(solution)/shard_map/ppermute | solution.py:19
  43.7 4.5 %collective-permute-start.1 = (f32[4,4,12,256]{3,2,1,0:T(8,128)S(1)}, f32[4,4,12,256]{3,2,1,0:T(8,128)S(1)}, u32[]{:S(2)}, u32[]{:S(2)}) collective-permute-start(f32[4,4,12,256]{3,2,1,0:T(8,128)S(1)} %get-tuple-element.9), channel_id=1, source_target_pairs={{0,1},{1,2},{2,3},{3,4},{4,5},{5,6},{6,7},{8,9},{9,10},{10,11},{11... | collective-permute-start | bytes 589832 | tf_op jit(solution)/shard_map/ppermute | solution.py:16
  65.5 10.4 %copy-start = (f32[4,4,24,256]{3,2,1,0:T(8,128)}, f32[4,4,24,256]{3,2,1,0:T(8,128)S(1)}, u32[]{:S(2)}) copy-start(f32[4,4,24,256]{3,2,1,0:T(8,128)S(1)} %divide_subtract_fusion) | copy-start | bytes 1179652
  65.6 6.3 %collective-permute-start.2 = (f32[4,4,12,256]{3,2,1,0:T(8,128)S(1)}, f32[4,4,12,256]{3,2,1,0:T(8,128)S(1)}, u32[]{:S(2)}, u32[]{:S(2)}) collective-permute-start(f32[4,4,12,256]{3,2,1,0:T(8,128)S(1)} %get-tuple-element.6), channel_id=1, source_target_pairs={{0,1},{1,2},{2,3},{3,4},{4,5},{5,6},{6,7},{8,9},{9,10},{10,11},{11... | collective-permute-start | bytes 589832 | tf_op jit(solution)/shard_map/ppermute | solution.py:16
  70.5 5.4 %collective-permute-start.3 = (f32[4,4,12,256]{3,2,1,0:T(8,128)S(1)}, f32[4,4,12,256]{3,2,1,0:T(8,128)S(1)}, u32[]{:S(2)}, u32[]{:S(2)}) collective-permute-start(f32[4,4,12,256]{3,2,1,0:T(8,128)S(1)} %get-tuple-element.7), channel_id=1, source_target_pairs={{1,0},{2,1},{3,2},{4,3},{5,4},{6,5},{7,6},{9,8},{10,9},{11,10},{12... | collective-permute-start | bytes 589832 | tf_op jit(solution)/shard_map/ppermute | solution.py:19
Sparse Core Ops, SparseCore 0:
  114.0 27.8 reduce-scatter.3
where the time goes:
time: 150 us; the launch traced here: 149 us
  matrix products  51.1 us (34%)
  waiting for transfers between devices  32.2 us (21%)
  other arithmetic  23.8 us (16%)
  between operations  14.3 us (10%)
  starting transfers between devices  10.8 us (7%)
  blocking collectives  10.6 us (7%)
  local copies, waits for them, and re-layouts  6.14 us (4%)
    dot_general x1, matrix products, on_device(): jnp.einsum('...m,mi->...i', lat_forward(widened, lat_taps), matrix, preci...  33.5 us
    unnamed x2, waiting for transfers between devices  28.1 us
    sub x1, other arithmetic, on_device(): updated = weights - STEP_RATE * grad_total / (1.0 + jnp.abs(grad_total))  17.3 us
    dot_general x1, matrix products, on_device(): jnp.einsum('...m,im->...i', products, matrix, precision=lax.Precision.HIG...  16.7 us
    all_gather x1, blocking collectives, on_device(): slot_blocks = lax.all_gather(gradient, 'mem', axis=1, tiled=True)  10.6 us
    ppermute x2, starting transfers between devices, with_halo(): lax.ppermute(lax.slice_in_dim(block, block.shape[dim] - width, None, axis...  8.02 us
    add x2, other arithmetic, level_filter(): result + tap_weights[position] * lax.slice_in_dim(padded, start_level, st...  6.42 us
    ppermute x2, waiting for transfers between devices, with_halo(): lax.ppermute(lax.slice_in_dim(block, 0, width, axis=dim), axis, backward)  4.09 us
  transfers between devices with their start and end apart: 5, of which 2 were waited for; matrix products, arithmetic and copies ran while one was open for 1% of the time, Pallas kernels for 0%

commit v1 on v0

v1 whole, which is shorter than its diff:
```python
import functools
import math

import jax
import jax.numpy as jnp
from jax import lax
from jax.experimental import pallas as pl
from jax.experimental.pallas import tpu as pltpu
from jax.sharding import PartitionSpec as P

STEP_RATE = 0.5
TILE = 8
F32 = jnp.float32
BF16 = jnp.bfloat16


def partner(me, d, n):
    if n & (n - 1):
        return (me + d) % n
    result = 0
    bit = 1
    while bit < n:
        result = result + ((me // bit + d // bit) % 2) * bit
        bit *= 2
    return result


def split(x):
    high = x.astype(BF16)
    return high, (x - high.astype(F32)).astype(BF16)


def dot(a, b, flip=False):
    dims = (((1,), (1 if flip else 0,)), ((), ()))
    return lax.dot_general(a, b, dims, preferred_element_type=F32)


def block_of(index, size, count):
    result = jnp.zeros_like(index)
    for i in range(1, count):
        result = result + (index >= i * size).astype(jnp.int32)
    return result


def kernel(
    n, bands, norm, radius, lev_width,
    g_hbm, p_hbm, w_hbm, lon_t, lat_t, lev_t, order,
    upd_hbm, inc_hbm,
    g_all, p_ref, w_ref, x_ref, u_ref, snd1, rcv1, snd2, rcv2, inc_ref, rs_ref, out_ref,
    c_hi, c_lo, k1_hi, k1_lo, k2_hi, k2_lo,
    load_sem, store_sem, gs, gr, h1s, h1r, h2s, h2r, rss, rsr,
):
    me = lax.axis_index("mem")
    band = lax.axis_index("lat")
    members, _, levels, rows, lons = p_ref.shape
    own_levels = g_hbm.shape[1]
    width = 2 * radius + 1
    full = radius // TILE * TILE
    rem = radius - full
    halo = levels * radius
    fulls = levels * full
    has_low, has_high = band > 0, band < bands - 1

    load_g = pltpu.make_async_copy(g_hbm, g_all.at[0], load_sem.at[0])
    load_p = pltpu.make_async_copy(p_hbm, p_ref, load_sem.at[1])
    load_w = pltpu.make_async_copy(w_hbm, w_ref, load_sem.at[2])
    load_g.start()
    load_p.start()
    load_w.start()

    barrier = pltpu.get_barrier_semaphore()
    mesh_ids = pl.DeviceIdType.MESH
    for d in range(1, n):
        pl.semaphore_signal(
            barrier, inc=1, device_id=(partner(me, d, n), band), device_id_type=mesh_ids
        )

    @pl.when(has_low)
    def _():
        pl.semaphore_signal(barrier, inc=1, device_id=(me, band - 1), device_id_type=mesh_ids)

    @pl.when(has_high)
    def _():
        pl.semaphore_signal(barrier, inc=1, device_id=(me, band + 1), device_id_type=mesh_ids)

    @pl.when(band == 0)
    def _():
        for k in range(members):
            rcv1[k, 0] = jnp.zeros((halo, lons), F32)
            rcv2[k, 0] = jnp.zeros((halo, lons), F32)

    @pl.when(band == bands - 1)
    def _():
        for k in range(members):
            rcv1[k, 1] = jnp.zeros((halo, lons), F32)
            rcv2[k, 1] = jnp.zeros((halo, lons), F32)

    load_g.wait()
    neighbours = has_low.astype(jnp.int32) + has_high.astype(jnp.int32)
    pl.semaphore_wait(barrier, n - 1 + neighbours)

    gathers = []
    for d in range(1, n):
        gathers.append(
            pltpu.make_async_remote_copy(
                src_ref=g_all.at[0],
                dst_ref=g_all.at[d],
                send_sem=gs.at[d - 1],
                recv_sem=gr.at[d - 1],
                device_id=(partner(me, d, n), band),
                device_id_type=mesh_ids,
            )
        )
        gathers[-1].start()

    def source(d):
        return partner(me, d, n) if not n & (n - 1) else (me + n - d) % n

    level_of = [
        order[source(q // own_levels) * own_levels + q % own_levels] for q in range(levels)
    ]

    step = 4 * TILE

    def lon_rows(i, carry):
        first = pl.multiple_of(i * step, step)
        row = lax.broadcasted_iota(jnp.int32, (step, lons), 0) + first
        col = lax.broadcasted_iota(jnp.int32, (step, lons), 1)
        off = col - row + radius
        off = jnp.where(off < 0, off + lons, off)
        off = jnp.where(off >= lons, off - lons, off)
        value = jnp.zeros((step, lons), F32)
        for j in range(width):
            value = jnp.where(off == j, lon_t[j], value)
        high, low = split(value)
        c_hi[pl.ds(first, step), :] = high
        c_lo[pl.ds(first, step), :] = low
        return carry

    lax.fori_loop(0, lons // step, lon_rows, 0)

    total = levels * rows + 2 * halo
    row = lax.broadcasted_iota(jnp.int32, (rows, total), 0)
    col = lax.broadcasted_iota(jnp.int32, (rows, total), 1)
    in_own = col < levels * rows
    in_high = col >= levels * rows + halo
    edge = col - levels * rows - jnp.where(in_high, halo, 0)
    in_full = edge < fulls
    rest = edge - fulls
    lev_own = block_of(col, rows, levels)
    lev_full = block_of(edge, full, levels)
    lev_rest = block_of(rest, rem, levels)
    lev = jnp.where(in_own, lev_own, jnp.where(in_full, lev_full, lev_rest))
    at_full = edge - lev_full * full
    at_rest = rest - lev_rest * rem
    low_pos = jnp.where(in_full, at_full - full, at_rest - radius)
    high_pos = jnp.where(in_full, at_full + rows, at_rest + rows + full)
    pos = jnp.where(in_own, col - lev_own * rows, jnp.where(in_high, high_pos, low_pos))
    shift = pos - row
    lat_adj = jnp.zeros((rows, total), F32)
    lat_fwd = jnp.zeros((rows, total), F32)
    for j in range(width):
        lat_adj = jnp.where(shift == radius - j, lat_t[j], lat_adj)
        lat_fwd = jnp.where(shift == j - radius, lat_t[j], lat_fwd)
    coef = []
    for l in range(levels):
        coef.append([])
        for q in range(levels):
            tap = l - level_of[q] + lev_width // 2
            inside = (tap >= 0) & (tap < lev_width)
            value = lev_t[jnp.clip(tap, 0, lev_width - 1)]
            coef[l].append(jnp.where(inside, value, 0.0))
    for a in range(levels):
        adj_coef = jnp.zeros((rows, total), F32)
        fwd_coef = jnp.zeros((rows, total), F32)
        for b in range(levels):
            adj_coef = jnp.where(lev == b, coef[a][b], adj_coef)
            fwd_coef = jnp.where(lev == b, coef[b][a], fwd_coef)
        at = slice(a * rows, (a + 1) * rows)
        k1_hi[at], k1_lo[at] = split(lat_adj * adj_coef)
        k2_hi[at], k2_lo[at] = split(lat_fwd * fwd_coef)

    load_p.wait()
    load_w.wait()

    def pert(k, v, q):
        return p_ref[k, v, level_of[q]].astype(F32)

    for q in range(levels):
        d, j = divmod(q, own_levels)
        if d and not j:
            gathers[d - 1].wait_recv()
        g0 = g_all[d, 0, j] * norm
        g1 = g_all[d, 1, j] * norm
        for k in range(members):
            x_ref[k, q * rows:(q + 1) * rows] = pert(k, 0, q) * g0 + pert(k, 1, q) * g1

    def halo_copies(snd, rcv, ss, rs, k):
        def make(side, target):
            return pltpu.make_async_remote_copy(
                src_ref=snd.at[k, side],
                dst_ref=rcv.at[k, side],
                send_sem=ss.at[k, side],
                recv_sem=rs.at[k, side],
                device_id=(me, target),
                device_id_type=mesh_ids,
            )

        return make(0, band + 1), make(1, band - 1)

    def send_halo(src, snd, rcv, ss, rs, k):
        for l in range(levels):
            base = l * rows
            snd[k, 0, l * full:(l + 1) * full] = src[k, base + rows - full:base + rows]
            snd[k, 1, l * full:(l + 1) * full] = src[k, base:base + full]
            at = slice(fulls + l * rem, fulls + (l + 1) * rem)
            snd[k, 0, at] = src[k, base + rows - radius:base + rows - full]
            snd[k, 1, at] = src[k, base + full:base + radius]
        up, down = halo_copies(snd, rcv, ss, rs, k)

        @pl.when(has_high)
        def _():
            up.start()

        @pl.when(has_low)
        def _():
            down.start()

    def wait_halo(snd, rcv, ss, rs, k):
        up, down = halo_copies(snd, rcv, ss, rs, k)

        @pl.when(has_low)
        def _():
            up.wait_recv()

        @pl.when(has_high)
        def _():
            down.wait_recv()

    def wait_sent(snd, rcv, ss, rs, k):
        up, down = halo_copies(snd, rcv, ss, rs, k)

        @pl.when(has_high)
        def _():
            up.wait_send()

        @pl.when(has_low)
        def _():
            down.wait_send()

    def apply(src, rcv, k, k_hi, k_lo, flip):
        x = jnp.concatenate([src[k], rcv[k, 0], rcv[k, 1]], axis=0)
        hi, lo = split(x)
        y = dot(k_hi[...], hi) + (dot(k_lo[...], hi) + dot(k_hi[...], lo))
        hi, lo = split(y)
        return dot(hi, c_hi[...], flip) + (dot(lo, c_hi[...], flip) + dot(hi, c_lo[...], flip))

    phase1 = (snd1, rcv1, h1s, h1r)
    phase2 = (snd2, rcv2, h2s, h2r)
    for k in range(members):
        send_halo(x_ref, *phase1, k)

    stores = []
    for k in range(members):
        wait_halo(*phase1, k)
        adjoint = apply(x_ref, rcv1, k, k1_hi, k1_lo, False)
        weight = w_ref[k]
        grad_total = weight + adjoint
        u_ref[k] = weight - STEP_RATE * grad_total / (1.0 + jnp.abs(grad_total))
        send_halo(u_ref, *phase2, k)
        stores.append(pltpu.make_async_copy(u_ref.at[k], upd_hbm.at[k], store_sem.at[k]))
        stores[-1].start()

    for k in range(members):
        wait_halo(*phase2, k)
        field = apply(u_ref, rcv2, k, k2_hi, k2_lo, True)
        for q in range(levels):
            d, j = divmod(q, own_levels)
            part = field[q * rows:(q + 1) * rows] * norm
            for v in range(2):
                term = pert(k, v, q) * part
                inc_ref[d, v, j] = term if k == 0 else inc_ref[d, v, j] + term

    scatters = []
    for d in range(n - 1, 0, -1):
        scatters.append(
            pltpu.make_async_remote_copy(
                src_ref=inc_ref.at[d],
                dst_ref=rs_ref.at[d - 1],
                send_sem=rss.at[d - 1],
                recv_sem=rsr.at[d - 1],
                device_id=(source(d), band),
                device_id_type=mesh_ids,
            )
        )
        scatters[-1].start()
    for copy in stores:
        copy.wait()
    for k in range(members):
        wait_sent(*phase1, k)
        wait_sent(*phase2, k)
    for copy in gathers:
        copy.wait_send()
    for copy in scatters:
        copy.wait_recv()
    result = inc_ref[0]
    for d in range(1, n):
        result = result + rs_ref[d - 1]
    out_ref[...] = result
    store = pltpu.make_async_copy(out_ref, inc_hbm, load_sem.at[0])
    store.start()
    for copy in scatters:
        copy.wait_send()
    store.wait()


def on_device(gradient, perturbations, weights, lon_taps, lat_taps, lev_taps, level_order):
    n, bands = lax.axis_size("mem"), lax.axis_size("lat")
    members, levels, rows, lons = weights.shape
    radius = lat_taps.shape[0] // 2
    norm = 1.0 / math.sqrt(members * n - 1)
    halo = levels * radius
    total = levels * rows + 2 * halo
    vmem, dma = pltpu.VMEM, pltpu.SemaphoreType.DMA
    anywhere = pl.BlockSpec(memory_space=pl.ANY)
    smem = pl.BlockSpec(memory_space=pltpu.SMEM)
    updated, increment = pl.pallas_call(
        functools.partial(kernel, n, bands, norm, radius, lev_taps.shape[0]),
        out_shape=(
            jax.ShapeDtypeStruct((members, levels * rows, lons), F32),
            jax.ShapeDtypeStruct(gradient.shape, F32),
        ),
        in_specs=[anywhere] * 3 + [smem] * 4,
        out_specs=(anywhere, anywhere),
        scratch_shapes=[
            vmem((n,) + gradient.shape, F32),
            vmem(perturbations.shape, BF16),
            vmem((members, levels * rows, lons), F32),
            vmem((members, levels * rows, lons), F32),
            vmem((members, levels * rows, lons), F32),
            vmem((members, 2, halo, lons), F32),
            vmem((members, 2, halo, lons), F32),
            vmem((members, 2, halo, lons), F32),
            vmem((members, 2, halo, lons), F32),
            vmem((n,) + gradient.shape, F32),
            vmem((n - 1,) + gradient.shape, F32),
            vmem(gradient.shape, F32),
            vmem((lons, lons), BF16),
            vmem((lons, lons), BF16),
            vmem((levels * rows, total), BF16),
            vmem((levels * rows, total), BF16),
            vmem((levels * rows, total), BF16),
            vmem((levels * rows, total), BF16),
            dma((3,)),
            dma((members,)),
            dma((n - 1,)),
            dma((n - 1,)),
            dma((members, 2)),
            dma((members, 2)),
            dma((members, 2)),
            dma((members, 2)),
            dma((n - 1,)),
            dma((n - 1,)),
        ],
        compiler_params=pltpu.CompilerParams(collective_id=0, has_side_effects=True),
        name="step",
    )(
        gradient,
        perturbations,
        weights.reshape(members, levels * rows, lons),
        lon_taps,
        lat_taps,
        lev_taps,
        level_order,
    )
    return updated.reshape(weights.shape), increment


def solution(mesh):
    in_specs = (
        P(None, "mem", "lat", None),
        P("mem", None, None, "lat", None),
        P("mem", None, "lat", None),
        P(),
        P(),
        P(),
        P(),
    )
    out_specs = (P("mem", None, "lat", None), P(None, "mem", "lat", None))
    return jax.shard_map(
        on_device, mesh=mesh, in_specs=in_specs, out_specs=out_specs, check_vma=False
    )
```

time: 150 us -> 24.2 us (0.16)
  matrix products: 51.1 us -> 0 us
  waiting for transfers between devices: 32.2 us -> 0 us
  other arithmetic: 23.8 us -> 0 us
  Pallas kernels: 0 us -> 21 us
  between operations: 14.3 us -> 0.65 us
  starting transfers between devices: 10.8 us -> 0 us
  blocking collectives: 10.6 us -> 0 us
  local copies, waits for them, and re-layouts: 6.14 us -> 2.41 us
    dot_general x4 -> x0, matrix products: 51.1 us -> none  [the longest x1 33.5 us: on_device(): jnp.einsum('...m,mi->...i', lat_forward(widened, lat_taps), matrix, preci...]
    unnamed x2 -> x0, waiting for transfers between devices: 28.1 us -> none
    pallas_call x0 -> x1, Pallas kernels: none -> 21 us  [on_device(): pl.pallas_call(functools.partial(kernel, n, bands, norm, radius, lev_taps...]
    sub x1 -> x0, other arithmetic: 17.3 us -> none  [on_device(): updated = weights - STEP_RATE * grad_total / (1.0 + jnp.abs(grad_total))]
    ppermute x4 -> x0, starting transfers between devices: 10.7 us -> none  [the longest x2 8.02 us: with_halo(): lax.ppermute(lax.slice_in_dim(block, block.shape[dim] - width, None, axis...]
    all_gather x1 -> x0, blocking collectives: 10.6 us -> none  [on_device(): slot_blocks = lax.all_gather(gradient, 'mem', axis=1, tiled=True)]
    add x2 -> x0, other arithmetic: 6.42 us -> none  [level_filter(): result + tap_weights[position] * lax.slice_in_dim(padded, start_level, st...]
    slice x7 -> x0, local copies, waits for them, and re-layouts: 4.43 us -> none  [the longest x2 2.3 us: circulant(): matrix = jnp.where(offsets == position, tap_weights[position], matrix)]
  transfers between devices with their start and end apart: 5 -> 0, of which waited for: 2 -> 0; matrix products, arithmetic and copies ran while one was open for 1% -> 0% of each run, Pallas kernels for 0% -> 0%
where the time goes in v1:
time: 24.2 us; the launch traced here: 24 us
  Pallas kernels  21 us (87%)
  local copies, waits for them, and re-layouts  2.41 us (10%)
  between operations  0.65 us (3%)
    pallas_call x1, Pallas kernels, on_device(): pl.pallas_call(functools.partial(kernel, n, bands, norm, radius, lev_taps...  21 us
    unnamed x4, local copies, waits for them, and re-layouts  2.41 us

profile of v1, /device:TPU:0, one launch (start us, length us, event | category | flops | bytes accessed | tf_op | source)
XLA Modules:
  0.0 24.0 jit_solution(4222941568175697728)
XLA Ops:
  0.6 21.0 %step.1 = (f32[4,96,256]{2,1,0:T(8,128)}, f32[2,1,24,256]{3,2,1,0:T(8,128)}) custom-call(f32[2,1,24,256]{3,2,1,0:T(8,128)} %g_hbm.1, bf16[4,2,4,24,256]{4,3,2,1,0:T(8,128)(2,1)} %p_hbm.1, f32[4,96,256]{2,1,0:T(8,128)} %bitcast.2, f32[25]{0:T(128)} %lon_t.1, f32[25]{0:T(128)} %lat_t.1, f32[5]{0:T(128)} %lev_t.1, s32[4]{0:T(128)} %order.1), custom_call_target="tpu_custom_call" | custom-call | tf_op jit(solution)/shard_map/step/pallas_call | solution.py:327
  21.6 0.0 copy-start
  21.6 1.8 %copy.11 = f32[4,4,24,256]{3,2,1,0:T(8,128)} copy(f32[4,4,24,256]{3,2,1,0:T(8,128)} %bitcast.3) | data formatting | bytes 786432
  23.4 0.0 copy-done
  23.4 0.6 %copy.12 = f32[2,1,24,256]{3,2,1,0:T(8,128)} copy(f32[2,1,24,256]{3,2,1,0:T(8,128)S(1)} %copy-done) | data formatting | bytes 98304
Async XLA Ops:
  21.6 1.8 %copy-start = (f32[2,1,24,256]{3,2,1,0:T(8,128)S(1)}, f32[2,1,24,256]{3,2,1,0:T(8,128)}, u32[]{:S(2)}) copy-start(f32[2,1,24,256]{3,2,1,0:T(8,128)} %get-tuple-element.9) | copy-start | bytes 147460

commit v2 on v1

--- a/solution.py
+++ b/solution.py
@@ -45,10 +45,10 @@
 def kernel(
     n, bands, norm, radius, lev_width,
     g_hbm, p_hbm, w_hbm, lon_t, lat_t, lev_t, order,
-    upd_hbm, inc_hbm,
-    g_all, p_ref, w_ref, x_ref, u_ref, snd1, rcv1, snd2, rcv2, inc_ref, rs_ref, out_ref,
+    u_ref, out_ref,
+    g_all, p_ref, w_ref, x_ref, snd1, rcv1, snd2, rcv2, inc_ref, rs_ref,
     c_hi, c_lo, k1_hi, k1_lo, k2_hi, k2_lo,
-    load_sem, store_sem, gs, gr, h1s, h1r, h2s, h2r, rss, rsr,
+    load_sem, gs, gr, h1s, h1r, h2s, h2r, rss, rsr,
 ):
     me = lax.axis_index("mem")
     band = lax.axis_index("lat")
@@ -260,7 +260,6 @@
     for k in range(members):
         send_halo(x_ref, *phase1, k)
 
-    stores = []
     for k in range(members):
         wait_halo(*phase1, k)
         adjoint = apply(x_ref, rcv1, k, k1_hi, k1_lo, False)
@@ -268,8 +267,6 @@
         grad_total = weight + adjoint
         u_ref[k] = weight - STEP_RATE * grad_total / (1.0 + jnp.abs(grad_total))
         send_halo(u_ref, *phase2, k)
-        stores.append(pltpu.make_async_copy(u_ref.at[k], upd_hbm.at[k], store_sem.at[k]))
-        stores[-1].start()
 
     for k in range(members):
         wait_halo(*phase2, k)
@@ -294,8 +291,6 @@
             )
         )
         scatters[-1].start()
-    for copy in stores:
-        copy.wait()
     for k in range(members):
         wait_sent(*phase1, k)
         wait_sent(*phase2, k)
@@ -307,11 +302,8 @@
     for d in range(1, n):
         result = result + rs_ref[d - 1]
     out_ref[...] = result
-    store = pltpu.make_async_copy(out_ref, inc_hbm, load_sem.at[0])
-    store.start()
     for copy in scatters:
         copy.wait_send()
-    store.wait()
 
 
 def on_device(gradient, perturbations, weights, lon_taps, lat_taps, lev_taps, level_order):
@@ -323,19 +315,19 @@
     total = levels * rows + 2 * halo
     vmem, dma = pltpu.VMEM, pltpu.SemaphoreType.DMA
     anywhere = pl.BlockSpec(memory_space=pl.ANY)
+    in_vmem = pl.BlockSpec(memory_space=pltpu.VMEM)
     smem = pl.BlockSpec(memory_space=pltpu.SMEM)
     updated, increment = pl.pallas_call(
         functools.partial(kernel, n, bands, norm, radius, lev_taps.shape[0]),
         out_shape=(
-            jax.ShapeDtypeStruct((members, levels * rows, lons), F32),
-            jax.ShapeDtypeStruct(gradient.shape, F32),
+            vmem((members, levels * rows, lons), F32),
+            vmem(gradient.shape, F32),
         ),
         in_specs=[anywhere] * 3 + [smem] * 4,
-        out_specs=(anywhere, anywhere),
+        out_specs=(in_vmem, in_vmem),
         scratch_shapes=[
             vmem((n,) + gradient.shape, F32),
             vmem(perturbations.shape, BF16),
-            vmem((members, levels * rows, lons), F32),
             vmem((members, levels * rows, lons), F32),
             vmem((members, levels * rows, lons), F32),
             vmem((members, 2, halo, lons), F32),
@@ -344,7 +336,6 @@
             vmem((members, 2, halo, lons), F32),
             vmem((n,) + gradient.shape, F32),
             vmem((n - 1,) + gradient.shape, F32),
-            vmem(gradient.shape, F32),
             vmem((lons, lons), BF16),
             vmem((lons, lons), BF16),
             vmem((levels * rows, total), BF16),
@@ -352,7 +343,6 @@
             vmem((levels * rows, total), BF16),
             vmem((levels * rows, total), BF16),
             dma((3,)),
-            dma((members,)),
             dma((n - 1,)),
             dma((n - 1,)),
             dma((members, 2)),

time: 24.2 us -> 22.5 us (0.930)
  local copies, waits for them, and re-layouts: 2.41 us -> 1.37 us
  Pallas kernels: 21 us -> 20.3 us
    unnamed x4 -> x2, local copies, waits for them, and re-layouts: 2.41 us -> 1.37 us
    pallas_call x1, Pallas kernels: 21 us -> 20.3 us  [on_device(): pl.pallas_call(functools.partial(kernel, n, bands, norm, radius, lev_taps...]
where the time goes in v2:
time: 22.5 us; the launch traced here: 22.4 us
  Pallas kernels  20.3 us (90%)
  local copies, waits for them, and re-layouts  1.37 us (6%)
  between operations  0.64 us (3%)
    pallas_call x1, Pallas kernels, on_device(): pl.pallas_call(functools.partial(kernel, n, bands, norm, radius, lev_taps...  20.3 us
    unnamed x2, local copies, waits for them, and re-layouts  1.37 us

profile of v2, /device:TPU:0, one launch (start us, length us, event | category | flops | bytes accessed | tf_op | source)
XLA Modules:
  0.0 22.4 jit_solution(705121972884989428)
XLA Ops:
  0.6 20.3 %step.1 = (f32[4,96,256]{2,1,0:T(8,128)S(1)}, f32[2,1,24,256]{3,2,1,0:T(8,128)S(1)}) custom-call(f32[2,1,24,256]{3,2,1,0:T(8,128)} %g_hbm.1, bf16[4,2,4,24,256]{4,3,2,1,0:T(8,128)(2,1)} %p_hbm.1, f32[4,96,256]{2,1,0:T(8,128)} %bitcast.3, f32[25]{0:T(128)} %lon_t.1, f32[25]{0:T(128)} %lat_t.1, f32[5]{0:T(128)} %lev_t.1, s32[4]{0:T(128)} %order.1), custom_call_target="tpu_custom_call" | custom-call | tf_op jit(solution)/shard_map/step/pallas_call | solution.py:320
  21.0 0.7 %copy.11 = f32[4,4,24,256]{3,2,1,0:T(8,128)} copy(f32[4,4,24,256]{3,2,1,0:T(8,128)S(1)} %bitcast.2) | data formatting | bytes 786432
  21.7 0.6 %copy.12 = f32[2,1,24,256]{3,2,1,0:T(8,128)} copy(f32[2,1,24,256]{3,2,1,0:T(8,128)S(1)} %get-tuple-element.7) | data formatting | bytes 98304

commit v3 on v2

--- a/solution.py
+++ b/solution.py
@@ -48,7 +48,7 @@
     u_ref, out_ref,
     g_all, p_ref, w_ref, x_ref, snd1, rcv1, snd2, rcv2, inc_ref, rs_ref,
     c_hi, c_lo, k1_hi, k1_lo, k2_hi, k2_lo,
-    load_sem, gs, gr, h1s, h1r, h2s, h2r, rss, rsr,
+    load_sem, known_sem, gs, gr, h1s, h1r, h2s, h2r, rss, rsr,
 ):
     me = lax.axis_index("mem")
     band = lax.axis_index("lat")
@@ -70,10 +70,16 @@
 
     barrier = pltpu.get_barrier_semaphore()
     mesh_ids = pl.DeviceIdType.MESH
-    for d in range(1, n):
-        pl.semaphore_signal(
-            barrier, inc=1, device_id=(partner(me, d, n), band), device_id_type=mesh_ids
-        )
+    cube = not n & (n - 1)
+    direct = [d for d in range(1, n) if not cube or not d & (d - 1)]
+
+    def greet(semaphore):
+        for d in direct:
+            pl.semaphore_signal(
+                semaphore, inc=1, device_id=(partner(me, d, n), band), device_id_type=mesh_ids
+            )
+
+    greet(barrier)
 
     @pl.when(has_low)
     def _():
@@ -97,12 +103,17 @@
 
     load_g.wait()
     neighbours = has_low.astype(jnp.int32) + has_high.astype(jnp.int32)
-    pl.semaphore_wait(barrier, n - 1 + neighbours)
-
-    gathers = []
-    for d in range(1, n):
-        gathers.append(
-            pltpu.make_async_remote_copy(
+    pl.semaphore_wait(barrier, len(direct) + neighbours)
+
+    gathers = {}
+    for hops in range(1, len(direct) + 1 if cube else 2):
+        if hops > 1:
+            greet(known_sem.at[hops - 2])
+            pl.semaphore_wait(known_sem.at[hops - 2], len(direct))
+        for d in range(1, n):
+            if cube and bin(d).count("1") != hops:
+                continue
+            gathers[d] = pltpu.make_async_remote_copy(
                 src_ref=g_all.at[0],
                 dst_ref=g_all.at[d],
                 send_sem=gs.at[d - 1],
@@ -110,8 +121,7 @@
                 device_id=(partner(me, d, n), band),
                 device_id_type=mesh_ids,
             )
-        )
-        gathers[-1].start()
+            gathers[d].start()
 
     def source(d):
         return partner(me, d, n) if not n & (n - 1) else (me + n - d) % n
@@ -189,7 +199,7 @@
     for q in range(levels):
         d, j = divmod(q, own_levels)
         if d and not j:
-            gathers[d - 1].wait_recv()
+            gathers[d].wait_recv()
         g0 = g_all[d, 0, j] * norm
         g1 = g_all[d, 1, j] * norm
         for k in range(members):
@@ -268,33 +278,33 @@
         u_ref[k] = weight - STEP_RATE * grad_total / (1.0 + jnp.abs(grad_total))
         send_halo(u_ref, *phase2, k)
 
+    scatters = []
     for k in range(members):
         wait_halo(*phase2, k)
         field = apply(u_ref, rcv2, k, k2_hi, k2_lo, True)
-        for q in range(levels):
-            d, j = divmod(q, own_levels)
-            part = field[q * rows:(q + 1) * rows] * norm
-            for v in range(2):
-                term = pert(k, v, q) * part
-                inc_ref[d, v, j] = term if k == 0 else inc_ref[d, v, j] + term
-
-    scatters = []
-    for d in range(n - 1, 0, -1):
-        scatters.append(
-            pltpu.make_async_remote_copy(
-                src_ref=inc_ref.at[d],
-                dst_ref=rs_ref.at[d - 1],
-                send_sem=rss.at[d - 1],
-                recv_sem=rsr.at[d - 1],
-                device_id=(source(d), band),
-                device_id_type=mesh_ids,
-            )
-        )
-        scatters[-1].start()
+        for d in range(n - 1, -1, -1):
+            for j in range(own_levels):
+                q = d * own_levels + j
+                part = field[q * rows:(q + 1) * rows] * norm
+                for v in range(2):
+                    term = pert(k, v, q) * part
+                    inc_ref[d, v, j] = term if k == 0 else inc_ref[d, v, j] + term
+            if d and k == members - 1:
+                scatters.append(
+                    pltpu.make_async_remote_copy(
+                        src_ref=inc_ref.at[d],
+                        dst_ref=rs_ref.at[d - 1],
+                        send_sem=rss.at[d - 1],
+                        recv_sem=rsr.at[d - 1],
+                        device_id=(source(d), band),
+                        device_id_type=mesh_ids,
+                    )
+                )
+                scatters[-1].start()
     for k in range(members):
         wait_sent(*phase1, k)
         wait_sent(*phase2, k)
-    for copy in gathers:
+    for copy in gathers.values():
         copy.wait_send()
     for copy in scatters:
         copy.wait_recv()
@@ -304,6 +314,15 @@
     out_ref[...] = result
     for copy in scatters:
         copy.wait_send()
+
+
+def write_out(u_ref, inc_ref, upd_hbm, inc_hbm, sem):
+    first = pltpu.make_async_copy(u_ref, upd_hbm, sem.at[0])
+    second = pltpu.make_async_copy(inc_ref, inc_hbm, sem.at[1])
+    first.start()
+    second.start()
+    first.wait()
+    second.wait()
 
 
 def on_device(gradient, perturbations, weights, lon_taps, lat_taps, lev_taps, level_order):
@@ -343,6 +362,7 @@
             vmem((levels * rows, total), BF16),
             vmem((levels * rows, total), BF16),
             dma((3,)),
+            pltpu.SemaphoreType.REGULAR((max(1, n.bit_length() - 2),)),
             dma((n - 1,)),
             dma((n - 1,)),
             dma((members, 2)),
@@ -363,6 +383,20 @@
         lev_taps,
         level_order,
     )
+    updated, increment = pl.pallas_call(
+        write_out,
+        out_shape=(
+            jax.ShapeDtypeStruct(updated.shape, F32),
+            jax.ShapeDtypeStruct(increment.shape, F32),
+        ),
+        in_specs=[in_vmem] * 2,
+        out_specs=(anywhere, anywhere),
+        scratch_shapes=[dma((2,))],
+        name="write_out",
+    )(
+        pltpu.with_memory_space_constraint(updated, pltpu.VMEM),
+        pltpu.with_memory_space_constraint(increment, pltpu.VMEM),
+    )
     return updated.reshape(weights.shape), increment
 
 

time: 22.5 us -> 22.1 us (0.982)
  local copies, waits for them, and re-layouts: 1.37 us -> 0 us
  Pallas kernels: 20.3 us -> 21.3 us
    unnamed x2 -> x0, local copies, waits for them, and re-layouts: 1.37 us -> none
    pallas_call x0 -> x1, Pallas kernels: none -> 0.77 us  [on_device(): pl.pallas_call(write_out, out_shape=(jax.ShapeDtypeStruct(updated.shape,...]
where the time goes in v3:
time: 22.1 us; the launch traced here: 21.9 us
  Pallas kernels  21.3 us (96%)
  between operations  0.64 us (3%)
    pallas_call x1, Pallas kernels, on_device(): pl.pallas_call(functools.partial(kernel, n, bands, norm, radius, lev_taps...  20.5 us
    pallas_call x1, Pallas kernels, on_device(): pl.pallas_call(write_out, out_shape=(jax.ShapeDtypeStruct(updated.shape,...  0.77 us

profile of v3, /device:TPU:0, one launch (start us, length us, event | category | flops | bytes accessed | tf_op | source)
XLA Modules:
  0.0 21.9 jit_solution(15730630058016274484)
XLA Ops:
  0.6 20.5 %step.1 = (f32[4,96,256]{2,1,0:T(8,128)S(1)}, f32[2,1,24,256]{3,2,1,0:T(8,128)S(1)}) custom-call(f32[2,1,24,256]{3,2,1,0:T(8,128)} %g_hbm.1, bf16[4,2,4,24,256]{4,3,2,1,0:T(8,128)(2,1)} %p_hbm.1, f32[4,96,256]{2,1,0:T(8,128)} %bitcast.2, f32[25]{0:T(128)} %lon_t.1, f32[25]{0:T(128)} %lat_t.1, f32[5]{0:T(128)} %lev_t.1, s32[4]{0:T(128)} %order.1), custom_call_target="tpu_custom_call" | custom-call | tf_op jit(solution)/shard_map/step/pallas_call | solution.py:339
  21.1 0.8 %write_out.1 = (f32[4,96,256]{2,1,0:T(8,128)}, f32[2,1,24,256]{3,2,1,0:T(8,128)}) custom-call(f32[4,96,256]{2,1,0:T(8,128)S(1)} %get-tuple-element.6.u_ref, f32[2,1,24,256]{3,2,1,0:T(8,128)S(1)} %get-tuple-element.7.inc_ref), custom_call_target="tpu_custom_call" | custom-call | tf_op jit(solution)/shard_map/write_out/pallas_call | solution.py:386
